TPU v7x, 32 devices: a whole 2x2x4 slice. The times are simulated.
32 devices in a mesh: tm: 16 (over z, x, core), space: 2 (over y).
Axes of the slice: x: 2, y: 2, z: 4, core: 2. Of those that a mesh axis runs over, the one named last changes fastest.
Arguments:
- nodes: float32 [16, 2, 2, 8, 128, 128], P('tm', None, None, 'space'), may hold values from -3 to 3
- initial: float32 [2, 8, 128, 128], P(None, 'space'), may hold values from -3 to 3
Outputs:
- corrected: float32 [16, 2, 2, 8, 128, 128], P('tm', None, None, 'space')
All inputs are finite; a program needn't handle non-finite values.
Results may differ from a plain program's by a relative error of at most 0.0003.
Values sent between devices are 32-bit elements; how exact they have to be, the bound alone decides.
No kernel may reach another device: no remote copies, remote signals or barrier semaphores. Data moves between devices by JAX's collectives and lax.ppermute only.
A program may use at most 128 MiB of HBM per device.

v0:
```python
import functools
import math

import jax
import jax.numpy as jnp
import numpy as np
from jax import lax
from jax.experimental import pallas as pl
from jax.experimental.pallas import tpu as pltpu
from jax.sharding import PartitionSpec as P

diffusion = (0.5, 0.25)
feed_rate = 0.04
kill_rate = 0.06
decay = (feed_rate, feed_rate + kill_rate)
slice_length = 0.5
node_step = 0.25
sweep_weights = ((5.0 / 24.0, 1.0 / 3.0, -1.0 / 24.0), (-1.0 / 24.0, 1.0 / 3.0, 5.0 / 24.0))
(T00, T01, T02), (T10, T11, T12) = [[slice_length * w for w in row] for row in sweep_weights]
AXES = ("tm", "space")
RIM = 8
TABLES = 6


def sine_table(points, modes):
    place = np.arange(points) + 0.5
    order = np.arange(modes) + 1.0
    weight = np.where(np.arange(modes) == modes - 1, math.sqrt(0.5), 1.0)
    return math.sqrt(2.0 / modes) * weight[None, :] * np.sin(math.pi / points * place[:, None] * order[None, :])


def np_split(table):
    table = np.asarray(table, np.float32)
    high = table.astype(jnp.bfloat16)
    low = (table - high.astype(np.float32)).astype(jnp.bfloat16)
    return high, low


def restricted(modes):
    return np.repeat(sine_table(modes, modes).T, 2, axis=1) * 0.5


def doubled(table):
    rows, columns = table.shape
    both = np.zeros((2 * rows, 2 * columns))
    both[:rows, :columns] = table
    both[rows:, columns:] = table
    return both


def eigen(count):
    return 2.0 * np.cos(math.pi * (np.arange(count) + 1.0) / count) - 2.0


def factor_table(modes_z, modes_x, modes_y):
    total = (eigen(modes_z)[:, None, None] + eigen(modes_x)[None, :, None] + eigen(modes_y)[None, None, :]) / 4.0
    linear = np.stack([diffusion[i] * total - decay[i] for i in range(2)], axis=2)
    factor = 1.0 / (1.0 - node_step * linear)
    return np.asarray(factor.reshape(modes_z * modes_x, 2 * modes_y), np.float32)


def split(table):
    high = table.astype(jnp.bfloat16)
    low = (table - high.astype(jnp.float32)).astype(jnp.bfloat16)
    return high, low


def dot(a, b):
    return jnp.dot(a, b, preferred_element_type=jnp.float32)


def pick(values, index):
    result = jnp.float32(values[0])
    for n, value in enumerate(values[1:], 1):
        result = jnp.where(index == n, jnp.float32(value), result)
    return result


def rates(p, q, near_p, near_q):
    reaction = (1.0 + p) * q * q
    return (
        diffusion[0] * near_p - (6.0 * diffusion[0] + decay[0]) * p - reaction,
        diffusion[1] * near_q - (6.0 * diffusion[1] + decay[1]) * q + reaction,
    )


def plane(ref, s, z):
    return ref[s, z, pl.ds(RIM, ref.shape[2] - 2 * RIM), :]


def in_plane(ref, s, z):
    rows, lanes = ref.shape[2] - 2 * RIM, ref.shape[3]
    v = plane(ref, s, z)
    lane = lax.broadcasted_iota(jnp.int32, (rows, lanes), 1)
    left = jnp.where(lane == lanes - 1, 0.0, pltpu.roll(v, lanes - 1, 1))
    right = jnp.where(lane == 0, 0.0, pltpu.roll(v, 1, 1))
    rims = ref[s, z, pl.ds(RIM - 1, rows), :] + ref[s, z, pl.ds(RIM + 1, rows), :]
    return rims + (left + right)


def rates_at(ref, z, around=None):
    planes = ref.shape[1]
    if around is None:
        around = [n for n in (z - 1, z + 1) if 0 <= n < planes]
    near = [sum((plane(ref, s, n) for n in around), in_plane(ref, s, z)) for s in range(2)]
    return rates(plane(ref, 0, z), plane(ref, 1, z), *near)


def set_plane(ref, s, z, value):
    ref[s, z, pl.ds(RIM, ref.shape[2] - 2 * RIM), :] = value


def clear_rims(ref):
    rows = ref.shape[2]
    zero = jnp.zeros((RIM, ref.shape[3]), jnp.float32)
    for s in range(2):
        for z in range(ref.shape[1]):
            ref[s, z, pl.ds(0, RIM), :] = zero
            ref[s, z, pl.ds(rows - RIM, RIM), :] = zero


def facing(spaces):
    if spaces == 2:
        return [1 - lax.axis_index("space")]
    return [0, 1]


def edge_plane(side, planes):
    return side * (planes - 1)


def edge_pair(side, planes):
    return side * (planes - 2)


def load_kernel(spaces, nodes, out, sem):
    planes = nodes.shape[3]
    place = edge_pair(facing(spaces)[0], planes) if spaces == 2 else 0
    copy = pltpu.make_async_copy(nodes.at[0, 1, :, pl.ds(place, out.shape[1])], out, sem.at[0])
    copy.start()
    copy.wait()


def early_kernel(spaces, nodes, *refs):
    sides = facing(spaces)
    tables, refs = refs[:TABLES], refs[TABLES:]
    one, rest, refs = refs[0], refs[1], refs[2:]
    outs, near, refs = refs[: len(sides)], refs[len(sides) : len(sides) + TABLES], refs[len(sides) + TABLES :]
    inner, (middle, finish, sems) = refs[:-3], refs[-3:]
    planes, rows = nodes.shape[3], nodes.shape[4]
    copies = [
        pltpu.make_async_copy(nodes.at[0, n], target.at[:, :, pl.ds(RIM, rows), :], sems.at[n])
        for n, target in enumerate((middle, finish))
    ]
    device = lax.axis_index("tm") * spaces + lax.axis_index("space")
    sources = [tables[0].at[device], *tables[1:]]
    others = [pltpu.make_async_copy(a, b, sems.at[2 + n]) for n, (a, b) in enumerate(zip(sources, near))]
    if inner:
        cut = pl.ds(2 - 2 * sides[0], planes - 2)
        others.append(pltpu.make_async_copy(nodes.at[0, 1, :, cut], inner[0], sems.at[2 + TABLES]))
    for copy in copies + others:
        copy.start()
    clear_rims(middle)
    clear_rims(finish)
    for copy in copies:
        copy.wait()
    for z in range(planes):
        f1, f2 = rates_at(middle, z), rates_at(finish, z)
        for s in range(2):
            one[s, z] = T01 * f1[s] + T02 * f2[s]
            rest[s, z] = (T11 - node_step) * f1[s] + T12 * f2[s]
    for side, out in zip(sides, outs):
        edge = edge_plane(side, planes)
        for s in range(2):
            mid, end = plane(middle, s, edge), plane(finish, s, edge)
            out[0, s] = T01 * mid + T02 * end
            out[1, s] = node_step * one[s, edge] + (T11 - node_step) * mid + T12 * end
    for copy in others:
        copy.wait()


def merge_kernel(spaces, initial, edge, *refs):
    count = 1 if spaces == 2 else 2
    owns, outs, (held, sem) = refs[:count], refs[count : 2 * count], refs[2 * count :]
    planes, rows = initial.shape[1], initial.shape[2]
    is_first = lax.axis_index("tm") == 0
    sides = facing(spaces)
    shift = edge_pair(sides[0], planes) if spaces == 2 else 0

    @pl.when(is_first)
    def _():
        copy = pltpu.make_async_copy(
            initial.at[:, pl.ds(shift, edge.shape[1])], held.at[:, :, pl.ds(RIM, rows), :], sem.at[0]
        )
        copy.start()
        copy.wait()

    @pl.when(jnp.logical_not(is_first))
    def _():
        for s in range(2):
            for z in range(edge.shape[1]):
                set_plane(held, s, z, edge[s, z])

    clear_rims(held)
    for side, own, out in zip(sides, owns, outs):
        first = edge_plane(side, planes) - shift
        second = first + 1 - 2 * side
        slope = rates_at(held, first, [second])
        for s in range(2):
            start = plane(held, s, first)
            out[0, s] = own[0, s] + T00 * start
            out[1, s] = own[1, s] + (node_step + T10) * start + (node_step * T00) * slope[s]


def start_kernel(spaces, initial, *refs):
    parts, refs = refs[: 2 if spaces == 2 else 1], refs[2 if spaces == 2 else 1 :]
    one_in, rest_in, start, one, rest, x_base, y_base, sem = refs
    planes, rows = initial.shape[1], initial.shape[2]
    is_first = lax.axis_index("tm") == 0

    @pl.when(is_first)
    def _():
        copy = pltpu.make_async_copy(initial, start.at[:, :, pl.ds(RIM, rows), :], sem.at[0])
        copy.start()
        copy.wait()

    @pl.when(jnp.logical_not(is_first))
    def _():
        if spaces == 2:
            side = facing(spaces)[0]
            places = [edge_pair(side, planes), 2 - 2 * side]
        else:
            places = [0]
        for place, part in zip(places, parts):
            for z in range(part.shape[1]):
                for s in range(2):
                    set_plane(start, s, place + z, part[s, z])

    clear_rims(start)
    for c in range(planes // 2):
        total = [0.0, 0.0]
        for z in (2 * c, 2 * c + 1):
            f0 = rates_at(start, z)
            for s in range(2):
                one[s, z] = plane(start, s, z) + T00 * f0[s] + one_in[s, z]
                rest[s, z] = T10 * f0[s] + rest_in[s, z]
                total[s] = total[s] + f0[s]
        for s in range(2):
            both = plane(start, s, 2 * c) + plane(start, s, 2 * c + 1)
            x_base[s, c] = (0.5 * T00) * total[s] + jnp.where(is_first, 0.5 * both, 0.0)
            y_base[s, c] = (0.5 * T10) * total[s]


def sweep_kernel(spaces, start, early, rest, x_base, y_base, *refs):
    sides = facing(spaces)
    count = len(sides)
    halos, owns, refs = refs[:count], refs[count : 2 * count], refs[2 * count :]
    table_x, table_y, table_f, one, two, element = refs[:6]
    targets, (slope1, stack, along, spec, x_part, y_part) = refs[6 : 6 + spaces], refs[6 + spaces :]
    planes = early.shape[1]
    half = planes // 2
    modes_x = table_x.shape[1]
    modes_z = table_f.shape[0] // modes_x
    rows, width_y = early.shape[2], early.shape[3]
    lanes = table_f.shape[1]
    me = lax.axis_index("space")
    clear_rims(one)
    clear_rims(two)
    for z in range(planes):
        for s in range(2):
            set_plane(one, s, z, early[s, z])
    for side, halo, own in zip(sides, halos, owns):
        edge = edge_plane(side, planes)
        for s in range(2):
            d = diffusion[s]
            set_plane(one, s, edge, plane(one, s, edge) + d * halo[0, s])
            back = T00 * plane(start, s, edge) + own[0, s]
            if spaces != 2:
                back = jnp.where(me == (0 if side == 0 else spaces - 1), 0.0, back)
            rest[s, edge] = rest[s, edge] + d * (halo[1, s] + (node_step * d) * back)
    for z in range(planes):
        g1 = rates_at(one, z)
        for s in range(2):
            first = plane(one, s, z)
            second = first + node_step * g1[s] + rest[s, z]
            set_plane(two, s, z, second)
            slope1[s, z // 2] = g1[s] if z % 2 == 0 else slope1[s, z // 2] + g1[s]

    def put(slot, s, value):
        stack[pl.ds(slot * rows, rows), pl.ds(s * width_y, width_y)] = value

    for n, side in enumerate(sides):
        edge = edge_plane(side, planes)
        for s in range(2):
            d = 0.5 * diffusion[s]
            zero, first, second = plane(start, s, edge), plane(one, s, edge), plane(two, s, edge)
            put(3 * half + 2 * n, s, d * (T00 * zero + T01 * first + T02 * second))
            put(3 * half + 2 * n + 1, s, d * (T10 * zero + T11 * first + T12 * second))
    for c in range(half):
        pair = [rates_at(two, 2 * c), rates_at(two, 2 * c + 1)]
        for s in range(2):
            g1, g2 = slope1[s, c], pair[0][s] + pair[1][s]
            first = 0.5 * (plane(one, s, 2 * c) + plane(one, s, 2 * c + 1))
            second = 0.5 * (plane(two, s, 2 * c) + plane(two, s, 2 * c + 1))
            put(c, s, x_base[s, c] + (0.5 * T01) * g1 + (0.5 * T02) * g2 - first)
            put(half + c, s, y_base[s, c] + (0.5 * T11) * g1 + (0.5 * T12) * g2 + (first - second))
            put(2 * half + c, s, second)
    fields = 3 * half + 2 * count
    for f in range(fields):
        high, low = split(stack[pl.ds(f * rows, rows), :])
        both = dot(high, table_y[...])
        along[:, pl.ds(f * lanes, lanes)] = both[:, :lanes] + (both[:, lanes:] + dot(low, table_y[:, :lanes]))
    for f in range(0, fields, 2):
        part = pl.ds(f * lanes, 2 * lanes)
        high, low = split(along[:, part])
        both = dot(table_x[...].reshape(2 * modes_x, rows), high)
        spec[:, part] = both[:modes_x] + (both[modes_x:] + dot(table_x[0], low))

    def at(f):
        return spec[:, pl.ds(f * lanes, lanes)]

    weights_z = sine_table(modes_z, modes_z)
    for k in range(modes_z):
        part = pl.ds(k * modes_x, modes_x)
        factor = table_f[part, :]
        weights = [pick([weights_z[d * half + c, k] for d in range(spaces)], me) for c in range(half)]
        x = sum(weights[c] * at(c) for c in range(half))
        y = sum(weights[c] * at(half + c) for c in range(half))
        e = sum(weights[c] * at(2 * half + c) for c in range(half))
        for n, side in enumerate(sides):
            below = [weights_z[d * half - 1, k] if d else 0.0 for d in range(spaces)]
            above = [weights_z[(d + 1) * half, k] if d < spaces - 1 else 0.0 for d in range(spaces)]
            weight = pick([b if d else a for d, (a, b) in enumerate(zip(above, below))] if spaces == 2 else (below, above)[side], me)
            x = x + weight * at(3 * half + 2 * n)
            y = y + weight * at(3 * half + 2 * n + 1)
        x = factor * x
        y = factor * (x + y)
        x_part[part, :] = x
        y_part[part, :] = y
        element[part, :] = y + e
    table = sine_table(planes * spaces, modes_z)
    for j, target in enumerate(targets):
        device = lax.rem(me + j, spaces)
        for z in range(planes):
            weights = [pick([table[d * planes + z, k] for d in range(spaces)], device) for k in range(modes_z)]
            for node, source in enumerate((x_part, y_part)):
                target[node, z] = sum(w * source[pl.ds(k * modes_x, modes_x), :] for k, w in enumerate(weights))


def chain_kernel(count, spaces, pieces, factor, *refs):
    out = refs[-1]
    gain = factor[...] * factor[...]
    state = jnp.zeros_like(gain)
    for t in range(count):
        for s in range(spaces):
            out[t * spaces + s] = state
        if t < count - 1:
            total = pieces[t * spaces]
            for s in range(1, spaces):
                total = total + pieces[t * spaces + s]
            state = gain * state + total


def finish_kernel(spaces, carried, one, two, keep, *refs):
    received = refs[: spaces - 1]
    table_x, table_y, table_f, out, left, right, wide, result, sems = refs[spaces - 1 :]
    planes, modes_x, lanes = keep.shape[1:]
    modes_z = table_f.shape[0] // modes_x
    width_y = out.shape[5]
    me = lax.axis_index("space")
    table = sine_table(planes * spaces, modes_z)
    for k in range(modes_z):
        part = pl.ds(k * modes_x, modes_x)
        left[part, :] = table_f[part, :] * carried[part, :]
        right[part, :] = table_f[part, :] * left[part, :]
    copies = []
    for node, source in ((0, left), (1, right)):
        for z in range(planes):
            value = keep[node, z]
            for other in received:
                value = value + other[node, z]
            for k in range(modes_z):
                weight = pick([table[d * planes + z, k] for d in range(spaces)], me)
                value = value + weight * source[pl.ds(k * modes_x, modes_x), :]
            high, low = split(value)
            wide[node * planes + z] = dot(jnp.concatenate([high, low], axis=1), table_y[0]) + dot(
                high, table_y[1, :lanes]
            )
    for node, swept in ((0, one), (1, two)):
        for z in range(planes):
            high, low = split(wide[node * planes + z])
            fine = dot(table_x[...], jnp.concatenate([high, high, low], axis=0))
            for s in range(2):
                result[node, s, z] = plane(swept, s, z) + fine[:, s * width_y : (s + 1) * width_y]
            copy = pltpu.make_async_copy(result.at[node, :, z], out.at[0, node, :, z], sems.at[node * planes + z])
            copy.start()
            copies.append(copy)
    for copy in copies:
        copy.wait()


def iteration(nodes, initial):
    count, spaces = lax.axis_size("tm"), lax.axis_size("space")
    planes, width_x, width_y = initial.shape[1:]
    modes_x, modes_y, modes_z = width_x // 2, width_y // 2, planes * spaces // 2
    half, lanes = planes // 2, 2 * modes_y
    devices = count * spaces
    f32 = jnp.float32
    shape = jax.ShapeDtypeStruct
    vmem, far = pl.BlockSpec(memory_space=pltpu.VMEM), pl.BlockSpec(memory_space=pltpu.HBM)
    params = pltpu.CompilerParams(vmem_limit_bytes=24 << 20)
    sides = 1 if spaces == 2 else 2
    sem = pltpu.SemaphoreType.DMA

    def in_hbm(value):
        return pltpu.with_memory_space_constraint(jnp.asarray(value), pltpu.HBM)

    nodes, initial = in_hbm(nodes), in_hbm(initial)
    rows = modes_z * modes_x
    share = rows // devices
    factors = factor_table(modes_z, modes_x, modes_y)
    high_x, low_x = np_split(sine_table(width_x, modes_x))
    high_y, low_y = np_split(doubled(sine_table(width_y, modes_y).T))
    tables = [
        factors.reshape(devices, share, lanes),
        np.stack(np_split(restricted(modes_x))),
        np.concatenate(np_split(doubled(restricted(modes_y).T)), axis=1),
        factors,
        np.concatenate([high_x, low_x, high_x], axis=1),
        np.stack([np.concatenate([high_y, high_y]), np.concatenate([low_y, low_y])]),
    ]
    near = [shape((share, lanes), f32)] + [shape(table.shape, table.dtype) for table in tables[1:]]

    plane_pair = shape((2, 2, width_x, width_y), f32)
    whole = shape((2, planes, width_x, width_y), f32)
    rimmed = shape((2, planes, width_x + 2 * RIM, width_y), f32)
    cuts = [2, planes - 2] if spaces == 2 else [planes]
    edge = pl.pallas_call(
        functools.partial(load_kernel, spaces),
        out_shape=shape((2, cuts[0], width_x, width_y), f32),
        in_specs=[far],
        out_specs=vmem,
        scratch_shapes=[sem((1,))],
        compiler_params=params,
        name="load",
    )(nodes)
    onward = [(t, t + 1) for t in range(count - 1)]
    parts = [lax.ppermute(edge, "tm", onward)]
    one, rest, *others = pl.pallas_call(
        functools.partial(early_kernel, spaces),
        out_shape=[whole] * 2
        + [plane_pair] * sides
        + near
        + [shape((2, cut, width_x, width_y), f32) for cut in cuts[1:]],
        in_specs=[far] * (1 + TABLES),
        out_specs=[vmem] * (2 + sides + TABLES + len(cuts) - 1),
        scratch_shapes=[pltpu.VMEM(rimmed.shape, f32)] * 2 + [sem((3 + TABLES,))],
        compiler_params=params,
        name="early",
    )(nodes, *[in_hbm(table) for table in tables])
    owns, near, inner = others[:sides], others[sides : sides + TABLES], others[sides + TABLES :]
    parts += [lax.ppermute(part, "tm", onward) for part in inner]
    merged = pl.pallas_call(
        functools.partial(merge_kernel, spaces),
        out_shape=[plane_pair] * sides,
        in_specs=[far] + [vmem] * (1 + sides),
        out_specs=[vmem] * sides,
        scratch_shapes=[pltpu.VMEM((2, cuts[0], width_x + 2 * RIM, width_y), f32), sem((1,))],
        compiler_params=params,
        name="merge",
    )(initial, parts[0], *owns)
    halos = []
    for n, part in enumerate(merged):
        if spaces == 2:
            moves = [(0, 1), (1, 0)]
        else:
            step = -1 if n == 0 else 1
            moves = [(s, s + step) for s in range(spaces) if 0 <= s + step < spaces]
        halos.append(lax.ppermute(part, "space", moves))
    if spaces != 2:
        halos = halos[::-1]
    start, one, rest, *bases = pl.pallas_call(
        functools.partial(start_kernel, spaces),
        out_shape=[rimmed] + [whole] * 2 + [shape((2, half, width_x, width_y), f32)] * 2,
        in_specs=[far] + [vmem] * (len(cuts) + 2),
        out_specs=[vmem] * 5,
        scratch_shapes=[sem((1,))],
        compiler_params=params,
        name="begin",
    )(initial, *parts, one, rest)

    block = shape((2, planes, modes_x, lanes), f32)
    fields = 3 * half + 2 * sides
    one, two, element, keep, *sends = pl.pallas_call(
        functools.partial(sweep_kernel, spaces),
        out_shape=[rimmed] * 2 + [shape((rows, lanes), f32)] + [block] * spaces,
        in_specs=[vmem] * (5 + 2 * sides + 3),
        out_specs=[vmem] * (3 + spaces),
        scratch_shapes=[
            pltpu.VMEM((2, half, width_x, width_y), f32),
            pltpu.VMEM((fields * width_x, 2 * width_y), f32),
            pltpu.VMEM((width_x, fields * lanes), f32),
            pltpu.VMEM((modes_x, fields * lanes), f32),
            pltpu.VMEM((rows, lanes), f32),
            pltpu.VMEM((rows, lanes), f32),
        ],
        compiler_params=params,
        name="sweep",
    )(start, one, rest, *bases, *halos, *owns, *near[1:4])

    received = []
    for j, send in enumerate(sends, 1):
        received.append(lax.ppermute(send, "space", [(s, (s + j) % spaces) for s in range(spaces)]))
    pieces = lax.all_to_all(element.reshape(devices, share, lanes), AXES, 0, 0, tiled=True)
    carried = pl.pallas_call(
        functools.partial(chain_kernel, count, spaces),
        out_shape=shape((devices, share, lanes), f32),
        in_specs=[vmem, vmem] + [pl.BlockSpec(memory_space=pl.ANY)] * (spaces - 1),
        out_specs=vmem,
        compiler_params=params,
        name="chain",
    )(pieces, near[0], *received)
    carried = lax.all_to_all(carried, AXES, 0, 0, tiled=True).reshape(rows, lanes)

    return pl.pallas_call(
        functools.partial(finish_kernel, spaces),
        out_shape=shape((1, 2, 2, planes, width_x, width_y), f32),
        in_specs=[vmem] * (4 + spaces - 1 + 3),
        out_specs=far,
        scratch_shapes=[pltpu.VMEM((rows, lanes), f32)] * 2
        + [
            pltpu.VMEM((2 * planes, modes_x, 2 * width_y), f32),
            pltpu.VMEM((2, 2, planes, width_x, width_y), f32),
            sem((2 * planes,)),
        ],
        compiler_params=params,
        name="finish",
    )(carried, one, two, keep, *received, near[4], near[5], near[3])


def solution(mesh):
    in_specs = (P("tm", None, None, "space", None, None), P(None, "space", None, None))
    out_specs = P("tm", None, None, "space", None, None)
    return jax.shard_map(iteration, mesh=mesh, in_specs=in_specs, out_specs=out_specs, check_vma=False)
```

profile of v0, /device:TPU:0, one launch (start us, length us, event | category | flops | bytes accessed | tf_op | source)
XLA Modules:
  0.0 45.8 jit_solution(10262017743452621148)
XLA Ops:
  0.0 1.0 %load.1 = f32[2,2,128,128]{3,2,1,0:T(8,128)S(1)} custom-call(f32[1,2,2,4,128,128]{5,4,3,2,1,0:T(8,128)} %nodes.3), custom_call_target="tpu_custom_call" | custom-call | tf_op jit(solution)/shard_map/load/pallas_call | solution.py:438
  1.0 2.4 %collective-permute-start = (f32[2,2,128,128]{3,2,1,0:T(8,128)S(1)}, f32[2,2,128,128]{3,2,1,0:T(8,128)S(1)}, u32[]{:S(2)}, u32[]{:S(2)}) collective-permute-start(f32[2,2,128,128]{3,2,1,0:T(8,128)S(1)} %load.1), channel_id=1, source_target_pairs={{0,2},{2,4},{4,6},{6,8},{8,10},{10,12},{12,14},{14,16},{16,18},{18... | collective-permute-start | bytes 786440 | tf_op jit(solution)/shard_map/ppermute | solution.py:448
  3.4 2.1 %early.1 = (f32[2,4,128,128]{3,2,1,0:T(8,128)S(1)}, f32[2,4,128,128]{3,2,1,0:T(8,128)S(1)}, f32[2,2,128,128]{3,2,1,0:T(8,128)S(1)}, f32[8,128]{1,0:T(8,128)S(1)}...) custom-call(f32[1,2,2,4,128,128]{5,4,3,2,1,0:T(8,128)} %nodes.3, ...), custom_call_target="tpu_custom_call" | custom-call | tf_op jit(solution)/shard_map/early/pallas_call | solution.py:449
  5.5 4.5 %collective-permute-start.1 = (f32[2,2,128,128]{3,2,1,0:T(8,128)S(1)}, f32[2,2,128,128]{3,2,1,0:T(8,128)S(1)}, u32[]{:S(2)}, u32[]{:S(2)}) collective-permute-start(f32[2,2,128,128]{3,2,1,0:T(8,128)S(1)} %get-tuple-element.25), channel_id=1, source_target_pairs={{0,2},{2,4},{4,6},{6,8},{8,10},{10,12},{12,14},{14,16},{16,18},{18... | collective-permute-start | bytes 786440 | tf_op jit(solution)/shard_map/ppermute | solution.py:462
  10.0 0.0 collective-permute-done.refs_0_.edge
  10.0 1.1 %merge.1 = f32[2,2,128,128]{3,2,1,0:T(8,128)S(1)} custom-call(f32[2,4,128,128]{3,2,1,0:T(8,128)} %initial.3, f32[2,2,128,128]{3,2,1,0:T(8,128)S(1)} %collective-permute-done.refs_0_.edge, f32[2,2,128,128]{3,2,1,0:T(8,128)S(1)} %get-tuple-element.33.refs_0_.refs_1_), custom_call_target="tpu_custom_call" | custom-call | tf_op jit(solution)/shard_map/merge/pallas_call | solution.py:463
  11.2 1.6 %collective-permute-start.2 = (f32[2,2,128,128]{3,2,1,0:T(8,128)S(1)}, f32[2,2,128,128]{3,2,1,0:T(8,128)S(1)}, u32[]{:S(2)}, u32[]{:S(2)}) collective-permute-start(f32[2,2,128,128]{3,2,1,0:T(8,128)S(1)} %merge.1), channel_id=1, source_target_pairs={{0,1},{1,0},{2,3},{3,2},{4,5},{5,4},{6,7},{7,6},{8,9},{9,8},{10,11... | collective-permute-start | bytes 786440 | tf_op jit(solution)/shard_map/ppermute | solution.py:479
  12.7 0.0 collective-permute-done.1.refs_1_
  12.7 1.5 %begin.1 = (f32[2,4,144,128]{3,2,1,0:T(8,128)S(1)}, f32[2,4,128,128]{3,2,1,0:T(8,128)S(1)}, f32[2,4,128,128]{3,2,1,0:T(8,128)S(1)}, f32[2,2,128,128]{3,2,1,0:T(8,128)S(1)}, f32[2,2,128,128]{3,2,1,0:T(8,128)S(1)}) custom-call(f32[2,4,128,128]{3,2,1,0:T(8,128)} %initial.3, f32[2,2,128,128]{3,2,1,0:T(8,128)S(1)} %collective-permute-done.refs_0_.edge, ...), custom_call_target="tpu_custom_call" | custom-call | tf_op jit(solution)/shard_map/begin/pallas_call | solution.py:482
  14.2 4.3 %collective-permute-done.2.refs_0_ = f32[2,2,128,128]{3,2,1,0:T(8,128)S(1)} collective-permute-done((f32[2,2,128,128]{3,2,1,0:T(8,128)S(1)}, f32[2,2,128,128]{3,2,1,0:T(8,128)S(1)}, u32[]{:S(2)}, u32[]{:S(2)}) %collective-permute-start.2) | collective-permute-done | bytes 262176 | tf_op jit(solution)/shard_map/ppermute | solution.py:479
  18.5 1.6 %sweep.1 = (f32[2,4,144,128]{3,2,1,0:T(8,128)S(1)}, f32[2,4,144,128]{3,2,1,0:T(8,128)S(1)}, f32[256,128]{1,0:T(8,128)S(1)}, f32[2,4,64,128]{3,2,1,0:T(8,128)S(1)}, f32[2,4,64,128]{3,2,1,0:T(8,128)S(1)}) custom-call(f32[2,4,144,128]{3,2,1,0:T(8,128)S(1)} %get-tuple-element.28.start, f32[2,4,128,128]{3,2,1,0:T(8,128)S(1)} %get-tuple-element.29.early, ...), custom_call_target="tpu_custom_call" | custom-call | tf_op jit(solution)/shard_map/sweep/pallas_call | solution.py:494
  20.1 1.5 %collective-permute-start.3 = (f32[2,4,64,128]{3,2,1,0:T(8,128)S(1)}, f32[2,4,64,128]{3,2,1,0:T(8,128)S(1)}, u32[]{:S(2)}, u32[]{:S(2)}) collective-permute-start(f32[2,4,64,128]{3,2,1,0:T(8,128)S(1)} %get-tuple-element.39), channel_id=1, source_target_pairs={{0,1},{1,0},{2,3},{3,2},{4,5},{5,4},{6,7},{7,6},{8,9},{9,8},{10,11... | collective-permute-start | bytes 786440 | tf_op jit(solution)/shard_map/ppermute | solution.py:513
  21.6 12.4 %all_to_all.10.pieces = f32[32,8,128]{2,1,0:T(8,128)S(1)} all-to-all(f32[32,8,128]{2,1,0:T(8,128)S(1)} %bitcast.3), channel_id=1, replica_groups=mesh['tm'=16,'space'=2] {'tm','space'}, dimensions={0} | all-to-all | bytes 262144 | tf_op jit(solution)/shard_map/all_to_all | solution.py:514
  34.0 0.0 collective-permute-done.3.refs_0_
  34.0 10.3 %all_to_all.11 = f32[32,8,128]{2,1,0:T(8,128)S(1)} all-to-all(f32[32,8,128]{2,1,0:T(8,128)S(1)} %chain.1), channel_id=1, replica_groups=mesh['tm'=16,'space'=2] {'tm','space'}, dimensions={0} | all-to-all | bytes 262144 | tf_op jit(solution)/shard_map/all_to_all | solution.py:523
  44.3 1.5 %finish.1 = f32[1,2,2,4,128,128]{5,4,3,2,1,0:T(8,128)} custom-call(f32[256,128]{1,0:T(8,128)S(1)} %bitcast.2, f32[2,4,144,128]{3,2,1,0:T(8,128)S(1)} %get-tuple-element.40.one, f32[2,4,144,128]{3,2,1,0:T(8,128)S(1)} %get-tuple-element.41.two, f32[2,4,64,128]{3,2,1,0:T(8,128)S(1)} %get-tuple-element.42.keep, ...), custom_call_target="tpu_custom_call" | custom-call | tf_op jit(solution)/shard_map/finish/pallas_call | solution.py:525
  (1 shorter events, 0.0 us)
Async XLA Ops:
  1.0 9.0 %collective-permute-start = (f32[2,2,128,128]{3,2,1,0:T(8,128)S(1)}, f32[2,2,128,128]{3,2,1,0:T(8,128)S(1)}, u32[]{:S(2)}, u32[]{:S(2)}) collective-permute-start(f32[2,2,128,128]{3,2,1,0:T(8,128)S(1)} %load.1), channel_id=1, source_target_pairs={{0,2},{2,4},{4,6},{6,8},{8,10},{10,12},{12,14},{14,16},{16,18},{18... | collective-permute-start | bytes 786440 | tf_op jit(solution)/shard_map/ppermute | solution.py:448
  5.5 7.2 %collective-permute-start.1 = (f32[2,2,128,128]{3,2,1,0:T(8,128)S(1)}, f32[2,2,128,128]{3,2,1,0:T(8,128)S(1)}, u32[]{:S(2)}, u32[]{:S(2)}) collective-permute-start(f32[2,2,128,128]{3,2,1,0:T(8,128)S(1)} %get-tuple-element.25), channel_id=1, source_target_pairs={{0,2},{2,4},{4,6},{6,8},{8,10},{10,12},{12,14},{14,16},{16,18},{18... | collective-permute-start | bytes 786440 | tf_op jit(solution)/shard_map/ppermute | solution.py:462
  11.2 7.3 %collective-permute-start.2 = (f32[2,2,128,128]{3,2,1,0:T(8,128)S(1)}, f32[2,2,128,128]{3,2,1,0:T(8,128)S(1)}, u32[]{:S(2)}, u32[]{:S(2)}) collective-permute-start(f32[2,2,128,128]{3,2,1,0:T(8,128)S(1)} %merge.1), channel_id=1, source_target_pairs={{0,1},{1,0},{2,3},{3,2},{4,5},{5,4},{6,7},{7,6},{8,9},{9,8},{10,11... | collective-permute-start | bytes 786440 | tf_op jit(solution)/shard_map/ppermute | solution.py:479
  20.1 13.9 %collective-permute-start.3 = (f32[2,4,64,128]{3,2,1,0:T(8,128)S(1)}, f32[2,4,64,128]{3,2,1,0:T(8,128)S(1)}, u32[]{:S(2)}, u32[]{:S(2)}) collective-permute-start(f32[2,4,64,128]{3,2,1,0:T(8,128)S(1)} %get-tuple-element.39), channel_id=1, source_target_pairs={{0,1},{1,0},{2,3},{3,2},{4,5},{5,4},{6,7},{7,6},{8,9},{9,8},{10,11... | collective-permute-start | bytes 786440 | tf_op jit(solution)/shard_map/ppermute | solution.py:513
where the time goes:
time: 46.1 us; the launch traced here: 45.8 us
  blocking collectives  22.7 us (49%)
  starting transfers between devices  10 us (22%)
  Pallas kernels  8.79 us (19%)
  waiting for transfers between devices  4.28 us (9%)
    all_to_all x1, blocking collectives, iteration(): lax.all_to_all(element.reshape(devices, share, lanes), AXES, 0, 0, tiled=...  12.4 us
    all_to_all x1, blocking collectives, iteration(): lax.all_to_all(carried, AXES, 0, 0, tiled=True).reshape(rows, lanes)  10.3 us
    ppermute x1, starting transfers between devices, iteration(): parts += [lax.ppermute(part, 'tm', onward) for part in inner]  4.5 us
    ppermute x1, waiting for transfers between devices, iteration(): halos.append(lax.ppermute(part, 'space', moves))  4.27 us
    ppermute x1, starting transfers between devices, iteration(): parts = [lax.ppermute(edge, 'tm', onward)]  2.41 us
    pallas_call x1, Pallas kernels, iteration(): pl.pallas_call(functools.partial(early_kernel, spaces), out_shape=[whole]...  2.1 us
    pallas_call x1, Pallas kernels, iteration(): pl.pallas_call(functools.partial(sweep_kernel, spaces), out_shape=[rimmed...  1.58 us
    ppermute x1, starting transfers between devices, iteration(): halos.append(lax.ppermute(part, 'space', moves))  1.55 us
  transfers between devices with their start and end apart: 4, of which 1 were waited for; matrix products, arithmetic and copies ran while one was open for 0% of the time, Pallas kernels for 10%

commit v1 on v0

--- a/solution.py
+++ b/solution.py
@@ -133,15 +133,30 @@
     return side * (planes - 2)
 
 
-def load_kernel(spaces, nodes, out, sem):
+def send_from(count, nodes, initial, cut, target, sem):
+    is_last = lax.axis_index("tm") == count - 1
+
+    def copy(source):
+        return pltpu.make_async_copy(source.at[:, cut], target, sem)
+
+    @pl.when(is_last)
+    def _():
+        copy(initial).start()
+
+    @pl.when(jnp.logical_not(is_last))
+    def _():
+        copy(nodes.at[0, 1]).start()
+
+    return copy(initial)
+
+
+def load_kernel(spaces, count, nodes, initial, out, sem):
     planes = nodes.shape[3]
     place = edge_pair(facing(spaces)[0], planes) if spaces == 2 else 0
-    copy = pltpu.make_async_copy(nodes.at[0, 1, :, pl.ds(place, out.shape[1])], out, sem.at[0])
-    copy.start()
-    copy.wait()
-
-
-def early_kernel(spaces, nodes, *refs):
+    send_from(count, nodes, initial, pl.ds(place, out.shape[1]), out, sem.at[0]).wait()
+
+
+def early_kernel(spaces, count, nodes, initial, *refs):
     sides = facing(spaces)
     tables, refs = refs[:TABLES], refs[TABLES:]
     one, rest, refs = refs[0], refs[1], refs[2:]
@@ -155,11 +170,11 @@
     device = lax.axis_index("tm") * spaces + lax.axis_index("space")
     sources = [tables[0].at[device], *tables[1:]]
     others = [pltpu.make_async_copy(a, b, sems.at[2 + n]) for n, (a, b) in enumerate(zip(sources, near))]
+    for copy in copies + others:
+        copy.start()
     if inner:
         cut = pl.ds(2 - 2 * sides[0], planes - 2)
-        others.append(pltpu.make_async_copy(nodes.at[0, 1, :, cut], inner[0], sems.at[2 + TABLES]))
-    for copy in copies + others:
-        copy.start()
+        others.append(send_from(count, nodes, initial, cut, inner[0], sems.at[2 + TABLES]))
     clear_rims(middle)
     clear_rims(finish)
     for copy in copies:
@@ -179,28 +194,14 @@
         copy.wait()
 
 
-def merge_kernel(spaces, initial, edge, *refs):
+def merge_kernel(spaces, planes, edge, *refs):
     count = 1 if spaces == 2 else 2
-    owns, outs, (held, sem) = refs[:count], refs[count : 2 * count], refs[2 * count :]
-    planes, rows = initial.shape[1], initial.shape[2]
-    is_first = lax.axis_index("tm") == 0
+    owns, outs, held = refs[:count], refs[count : 2 * count], refs[2 * count]
     sides = facing(spaces)
     shift = edge_pair(sides[0], planes) if spaces == 2 else 0
-
-    @pl.when(is_first)
-    def _():
-        copy = pltpu.make_async_copy(
-            initial.at[:, pl.ds(shift, edge.shape[1])], held.at[:, :, pl.ds(RIM, rows), :], sem.at[0]
-        )
-        copy.start()
-        copy.wait()
-
-    @pl.when(jnp.logical_not(is_first))
-    def _():
-        for s in range(2):
-            for z in range(edge.shape[1]):
-                set_plane(held, s, z, edge[s, z])
-
+    for s in range(2):
+        for z in range(edge.shape[1]):
+            set_plane(held, s, z, edge[s, z])
     clear_rims(held)
     for side, own, out in zip(sides, owns, outs):
         first = edge_plane(side, planes) - shift
@@ -212,30 +213,20 @@
             out[1, s] = own[1, s] + (node_step + T10) * start + (node_step * T00) * slope[s]
 
 
-def start_kernel(spaces, initial, *refs):
+def start_kernel(spaces, *refs):
     parts, refs = refs[: 2 if spaces == 2 else 1], refs[2 if spaces == 2 else 1 :]
-    one_in, rest_in, start, one, rest, x_base, y_base, sem = refs
-    planes, rows = initial.shape[1], initial.shape[2]
+    one_in, rest_in, start, one, rest, x_base, y_base = refs
+    planes = one.shape[1]
     is_first = lax.axis_index("tm") == 0
-
-    @pl.when(is_first)
-    def _():
-        copy = pltpu.make_async_copy(initial, start.at[:, :, pl.ds(RIM, rows), :], sem.at[0])
-        copy.start()
-        copy.wait()
-
-    @pl.when(jnp.logical_not(is_first))
-    def _():
-        if spaces == 2:
-            side = facing(spaces)[0]
-            places = [edge_pair(side, planes), 2 - 2 * side]
-        else:
-            places = [0]
-        for place, part in zip(places, parts):
-            for z in range(part.shape[1]):
-                for s in range(2):
-                    set_plane(start, s, place + z, part[s, z])
-
+    if spaces == 2:
+        side = facing(spaces)[0]
+        places = [edge_pair(side, planes), 2 - 2 * side]
+    else:
+        places = [0]
+    for place, part in zip(places, parts):
+        for z in range(part.shape[1]):
+            for s in range(2):
+                set_plane(start, s, place + z, part[s, z])
     clear_rims(start)
     for c in range(planes // 2):
         total = [0.0, 0.0]
@@ -436,39 +427,39 @@
     rimmed = shape((2, planes, width_x + 2 * RIM, width_y), f32)
     cuts = [2, planes - 2] if spaces == 2 else [planes]
     edge = pl.pallas_call(
-        functools.partial(load_kernel, spaces),
+        functools.partial(load_kernel, spaces, count),
         out_shape=shape((2, cuts[0], width_x, width_y), f32),
-        in_specs=[far],
+        in_specs=[far, far],
         out_specs=vmem,
         scratch_shapes=[sem((1,))],
         compiler_params=params,
         name="load",
-    )(nodes)
-    onward = [(t, t + 1) for t in range(count - 1)]
+    )(nodes, initial)
+    onward = [(t, (t + 1) % count) for t in range(count)]
     parts = [lax.ppermute(edge, "tm", onward)]
     one, rest, *others = pl.pallas_call(
-        functools.partial(early_kernel, spaces),
+        functools.partial(early_kernel, spaces, count),
         out_shape=[whole] * 2
         + [plane_pair] * sides
         + near
         + [shape((2, cut, width_x, width_y), f32) for cut in cuts[1:]],
-        in_specs=[far] * (1 + TABLES),
+        in_specs=[far] * (2 + TABLES),
         out_specs=[vmem] * (2 + sides + TABLES + len(cuts) - 1),
         scratch_shapes=[pltpu.VMEM(rimmed.shape, f32)] * 2 + [sem((3 + TABLES,))],
         compiler_params=params,
         name="early",
-    )(nodes, *[in_hbm(table) for table in tables])
+    )(nodes, initial, *[in_hbm(table) for table in tables])
     owns, near, inner = others[:sides], others[sides : sides + TABLES], others[sides + TABLES :]
     parts += [lax.ppermute(part, "tm", onward) for part in inner]
     merged = pl.pallas_call(
-        functools.partial(merge_kernel, spaces),
+        functools.partial(merge_kernel, spaces, planes),
         out_shape=[plane_pair] * sides,
-        in_specs=[far] + [vmem] * (1 + sides),
+        in_specs=[vmem] * (1 + sides),
         out_specs=[vmem] * sides,
-        scratch_shapes=[pltpu.VMEM((2, cuts[0], width_x + 2 * RIM, width_y), f32), sem((1,))],
+        scratch_shapes=[pltpu.VMEM((2, cuts[0], width_x + 2 * RIM, width_y), f32)],
         compiler_params=params,
         name="merge",
-    )(initial, parts[0], *owns)
+    )(parts[0], *owns)
     halos = []
     for n, part in enumerate(merged):
         if spaces == 2:
@@ -482,12 +473,11 @@
     start, one, rest, *bases = pl.pallas_call(
         functools.partial(start_kernel, spaces),
         out_shape=[rimmed] + [whole] * 2 + [shape((2, half, width_x, width_y), f32)] * 2,
-        in_specs=[far] + [vmem] * (len(cuts) + 2),
+        in_specs=[vmem] * (len(cuts) + 2),
         out_specs=[vmem] * 5,
-        scratch_shapes=[sem((1,))],
         compiler_params=params,
         name="begin",
-    )(initial, *parts, one, rest)
+    )(*parts, one, rest)
 
     block = shape((2, planes, modes_x, lanes), f32)
     fields = 3 * half + 2 * sides

time: 46.1 us -> 43.4 us (0.941)
  waiting for transfers between devices: 4.28 us -> 8.15 us
  starting transfers between devices: 10 us -> 7.45 us
  blocking collectives: 22.7 us -> 20.7 us
  Pallas kernels: 8.79 us -> 6.81 us
    ppermute x1, waiting for transfers between devices: 0.01 us -> 4.27 us  [iteration(): parts = [lax.ppermute(edge, 'tm', onward)]]
    all_to_all x1, blocking collectives: 12.4 us -> 10.4 us  [iteration(): lax.all_to_all(element.reshape(devices, share, lanes), AXES, 0, 0, tiled=...]
    ppermute x1, starting transfers between devices: 2.41 us -> 0.54 us  [iteration(): parts = [lax.ppermute(edge, 'tm', onward)]]
    ppermute x1, starting transfers between devices: 4.5 us -> 2.64 us  [iteration(): parts += [lax.ppermute(part, 'tm', onward) for part in inner]]
    pallas_call x1, Pallas kernels: 1.51 us -> 0.51 us  [iteration(): pl.pallas_call(functools.partial(start_kernel, spaces), out_shape=[rimmed...]
    ppermute x1, waiting for transfers between devices: 4.27 us -> 3.3 us  [iteration(): halos.append(lax.ppermute(part, 'space', moves))]
    pallas_call x3, Pallas kernels: 4.19 us -> 3.22 us  [the longest x1 2.08 us: iteration(): pl.pallas_call(functools.partial(early_kernel, spaces, count), out_shape=...]
    ppermute x1, starting transfers between devices: 1.53 us -> 2.22 us  [iteration(): lax.ppermute(send, 'space', [(s, (s + j) % spaces) for s in range(spaces)])]
  transfers between devices with their start and end apart: 4 -> 4, of which waited for: 1 -> 3; matrix products, arithmetic and copies ran while one was open for 0% -> 0% of each run, Pallas kernels for 10% -> 6%
where the time goes in v1:
time: 43.4 us; the launch traced here: 43.2 us
  blocking collectives  20.7 us (48%)
  waiting for transfers between devices  8.15 us (19%)
  starting transfers between devices  7.45 us (17%)
  Pallas kernels  6.81 us (16%)
    all_to_all x1, blocking collectives, iteration(): lax.all_to_all(element.reshape(devices, share, lanes), AXES, 0, 0, tiled=...  10.4 us
    all_to_all x1, blocking collectives, iteration(): lax.all_to_all(carried, AXES, 0, 0, tiled=True).reshape(rows, lanes)  10.3 us
    ppermute x1, waiting for transfers between devices, iteration(): parts = [lax.ppermute(edge, 'tm', onward)]  4.27 us
    ppermute x1, waiting for transfers between devices, iteration(): halos.append(lax.ppermute(part, 'space', moves))  3.3 us
    ppermute x1, starting transfers between devices, iteration(): parts += [lax.ppermute(part, 'tm', onward) for part in inner]  2.64 us
    ppermute x1, starting transfers between devices, iteration(): lax.ppermute(send, 'space', [(s, (s + j) % spaces) for s in range(spaces)])  2.22 us
    pallas_call x1, Pallas kernels, iteration(): pl.pallas_call(functools.partial(early_kernel, spaces, count), out_shape=...  2.08 us
    ppermute x1, starting transfers between devices, iteration(): halos.append(lax.ppermute(part, 'space', moves))  2.04 us
  transfers between devices with their start and end apart: 4, of which 3 were waited for; matrix products, arithmetic and copies ran while one was open for 0% of the time, Pallas kernels for 6%

profile of v1, /device:TPU:0, one launch (start us, length us, event | category | flops | bytes accessed | tf_op | source)
XLA Modules:
  0.0 43.2 jit_solution(13342398063608448983)
XLA Ops:
  0.0 1.0 %load.1 = f32[2,2,128,128]{3,2,1,0:T(8,128)S(1)} custom-call(f32[1,2,2,4,128,128]{5,4,3,2,1,0:T(8,128)} %nodes.3, f32[2,4,128,128]{3,2,1,0:T(8,128)} %initial.3), custom_call_target="tpu_custom_call" | custom-call | tf_op jit(solution)/shard_map/load/pallas_call | solution.py:429
  1.0 0.5 %collective-permute-start = (f32[2,2,128,128]{3,2,1,0:T(8,128)S(1)}, f32[2,2,128,128]{3,2,1,0:T(8,128)S(1)}, u32[]{:S(2)}, u32[]{:S(2)}) collective-permute-start(f32[2,2,128,128]{3,2,1,0:T(8,128)S(1)} %load.1), channel_id=1, source_target_pairs={{0,2},{2,4},{4,6},{6,8},{8,10},{10,12},{12,14},{14,16},{16,18},{18... | collective-permute-start | bytes 786440 | tf_op jit(solution)/shard_map/ppermute | solution.py:439
  1.5 2.1 %early.1 = (f32[2,4,128,128]{3,2,1,0:T(8,128)S(1)}, f32[2,4,128,128]{3,2,1,0:T(8,128)S(1)}, f32[2,2,128,128]{3,2,1,0:T(8,128)S(1)}, f32[8,128]{1,0:T(8,128)S(1)}...) custom-call(f32[1,2,2,4,128,128]{5,4,3,2,1,0:T(8,128)} %nodes.3, ...), custom_call_target="tpu_custom_call" | custom-call | tf_op jit(solution)/shard_map/early/pallas_call | solution.py:440
  3.6 2.6 %collective-permute-start.1 = (f32[2,2,128,128]{3,2,1,0:T(8,128)S(1)}, f32[2,2,128,128]{3,2,1,0:T(8,128)S(1)}, u32[]{:S(2)}, u32[]{:S(2)}) collective-permute-start(f32[2,2,128,128]{3,2,1,0:T(8,128)S(1)} %get-tuple-element.25), channel_id=1, source_target_pairs={{0,2},{2,4},{4,6},{6,8},{8,10},{10,12},{12,14},{14,16},{16,18},{18... | collective-permute-start | bytes 786440 | tf_op jit(solution)/shard_map/ppermute | solution.py:453
  6.2 4.3 %collective-permute-done.refs_0_.edge = f32[2,2,128,128]{3,2,1,0:T(8,128)S(1)} collective-permute-done((f32[2,2,128,128]{3,2,1,0:T(8,128)S(1)}, f32[2,2,128,128]{3,2,1,0:T(8,128)S(1)}, u32[]{:S(2)}, u32[]{:S(2)}) %collective-permute-start) | collective-permute-done | bytes 262176 | tf_op jit(solution)/shard_map/ppermute | solution.py:439
  10.5 0.2 merge.1
  10.7 2.0 %collective-permute-start.2 = (f32[2,2,128,128]{3,2,1,0:T(8,128)S(1)}, f32[2,2,128,128]{3,2,1,0:T(8,128)S(1)}, u32[]{:S(2)}, u32[]{:S(2)}) collective-permute-start(f32[2,2,128,128]{3,2,1,0:T(8,128)S(1)} %merge.1), channel_id=1, source_target_pairs={{0,1},{1,0},{2,3},{3,2},{4,5},{5,4},{6,7},{7,6},{8,9},{9,8},{10,11... | collective-permute-start | bytes 786440 | tf_op jit(solution)/shard_map/ppermute | solution.py:470
  12.7 0.6 %collective-permute-done.1.refs_1_ = f32[2,2,128,128]{3,2,1,0:T(8,128)S(1)} collective-permute-done((f32[2,2,128,128]{3,2,1,0:T(8,128)S(1)}, f32[2,2,128,128]{3,2,1,0:T(8,128)S(1)}, u32[]{:S(2)}, u32[]{:S(2)}) %collective-permute-start.1) | collective-permute-done | bytes 262176 | tf_op jit(solution)/shard_map/ppermute | solution.py:453
  13.3 0.5 %begin.1 = (f32[2,4,144,128]{3,2,1,0:T(8,128)S(1)}, f32[2,4,128,128]{3,2,1,0:T(8,128)S(1)}, f32[2,4,128,128]{3,2,1,0:T(8,128)S(1)}, f32[2,2,128,128]{3,2,1,0:T(8,128)S(1)}, f32[2,2,128,128]{3,2,1,0:T(8,128)S(1)}) custom-call(f32[2,2,128,128]{3,2,1,0:T(8,128)S(1)} %collective-permute-done.refs_0_.edge, f32[2,2,128,128]{3,2,1,0:T(8,128)S(1)} %collective-permute-done.1.refs_1_, ...), custom_call_target="tpu_custom_call" | custom-call | tf_op jit(solution)/shard_map/begin/pallas_call | solution.py:473
  13.8 3.3 %collective-permute-done.2.refs_0_ = f32[2,2,128,128]{3,2,1,0:T(8,128)S(1)} collective-permute-done((f32[2,2,128,128]{3,2,1,0:T(8,128)S(1)}, f32[2,2,128,128]{3,2,1,0:T(8,128)S(1)}, u32[]{:S(2)}, u32[]{:S(2)}) %collective-permute-start.2) | collective-permute-done | bytes 262176 | tf_op jit(solution)/shard_map/ppermute | solution.py:470
  17.1 1.6 %sweep.1 = (f32[2,4,144,128]{3,2,1,0:T(8,128)S(1)}, f32[2,4,144,128]{3,2,1,0:T(8,128)S(1)}, f32[256,128]{1,0:T(8,128)S(1)}, f32[2,4,64,128]{3,2,1,0:T(8,128)S(1)}, f32[2,4,64,128]{3,2,1,0:T(8,128)S(1)}) custom-call(f32[2,4,144,128]{3,2,1,0:T(8,128)S(1)} %get-tuple-element.28.start, f32[2,4,128,128]{3,2,1,0:T(8,128)S(1)} %get-tuple-element.29.early, ...), custom_call_target="tpu_custom_call" | custom-call | tf_op jit(solution)/shard_map/sweep/pallas_call | solution.py:484
  18.7 2.2 %collective-permute-start.3 = (f32[2,4,64,128]{3,2,1,0:T(8,128)S(1)}, f32[2,4,64,128]{3,2,1,0:T(8,128)S(1)}, u32[]{:S(2)}, u32[]{:S(2)}) collective-permute-start(f32[2,4,64,128]{3,2,1,0:T(8,128)S(1)} %get-tuple-element.39), channel_id=1, source_target_pairs={{0,1},{1,0},{2,3},{3,2},{4,5},{5,4},{6,7},{7,6},{8,9},{9,8},{10,11... | collective-permute-start | bytes 786440 | tf_op jit(solution)/shard_map/ppermute | solution.py:503
  21.0 10.4 %all_to_all.10.pieces = f32[32,8,128]{2,1,0:T(8,128)S(1)} all-to-all(f32[32,8,128]{2,1,0:T(8,128)S(1)} %bitcast.3), channel_id=1, replica_groups=mesh['tm'=16,'space'=2] {'tm','space'}, dimensions={0} | all-to-all | bytes 262144 | tf_op jit(solution)/shard_map/all_to_all | solution.py:504
  31.4 0.0 collective-permute-done.3.refs_0_
  31.4 10.3 %all_to_all.11 = f32[32,8,128]{2,1,0:T(8,128)S(1)} all-to-all(f32[32,8,128]{2,1,0:T(8,128)S(1)} %chain.1), channel_id=1, replica_groups=mesh['tm'=16,'space'=2] {'tm','space'}, dimensions={0} | all-to-all | bytes 262144 | tf_op jit(solution)/shard_map/all_to_all | solution.py:513
  41.7 1.5 %finish.1 = f32[1,2,2,4,128,128]{5,4,3,2,1,0:T(8,128)} custom-call(f32[256,128]{1,0:T(8,128)S(1)} %bitcast.2, f32[2,4,144,128]{3,2,1,0:T(8,128)S(1)} %get-tuple-element.40.one, f32[2,4,144,128]{3,2,1,0:T(8,128)S(1)} %get-tuple-element.41.two, f32[2,4,64,128]{3,2,1,0:T(8,128)S(1)} %get-tuple-element.42.keep, ...), custom_call_target="tpu_custom_call" | custom-call | tf_op jit(solution)/shard_map/finish/pallas_call | solution.py:515
  (1 shorter events, 0.0 us)
Async XLA Ops:
  1.0 9.6 %collective-permute-start = (f32[2,2,128,128]{3,2,1,0:T(8,128)S(1)}, f32[2,2,128,128]{3,2,1,0:T(8,128)S(1)}, u32[]{:S(2)}, u32[]{:S(2)}) collective-permute-start(f32[2,2,128,128]{3,2,1,0:T(8,128)S(1)} %load.1), channel_id=1, source_target_pairs={{0,2},{2,4},{4,6},{6,8},{8,10},{10,12},{12,14},{14,16},{16,18},{18... | collective-permute-start | bytes 786440 | tf_op jit(solution)/shard_map/ppermute | solution.py:439
  3.6 9.7 %collective-permute-start.1 = (f32[2,2,128,128]{3,2,1,0:T(8,128)S(1)}, f32[2,2,128,128]{3,2,1,0:T(8,128)S(1)}, u32[]{:S(2)}, u32[]{:S(2)}) collective-permute-start(f32[2,2,128,128]{3,2,1,0:T(8,128)S(1)} %get-tuple-element.25), channel_id=1, source_target_pairs={{0,2},{2,4},{4,6},{6,8},{8,10},{10,12},{12,14},{14,16},{16,18},{18... | collective-permute-start | bytes 786440 | tf_op jit(solution)/shard_map/ppermute | solution.py:453
  10.7 6.4 %collective-permute-start.2 = (f32[2,2,128,128]{3,2,1,0:T(8,128)S(1)}, f32[2,2,128,128]{3,2,1,0:T(8,128)S(1)}, u32[]{:S(2)}, u32[]{:S(2)}) collective-permute-start(f32[2,2,128,128]{3,2,1,0:T(8,128)S(1)} %merge.1), channel_id=1, source_target_pairs={{0,1},{1,0},{2,3},{3,2},{4,5},{5,4},{6,7},{7,6},{8,9},{9,8},{10,11... | collective-permute-start | bytes 786440 | tf_op jit(solution)/shard_map/ppermute | solution.py:470
  18.7 12.7 %collective-permute-start.3 = (f32[2,4,64,128]{3,2,1,0:T(8,128)S(1)}, f32[2,4,64,128]{3,2,1,0:T(8,128)S(1)}, u32[]{:S(2)}, u32[]{:S(2)}) collective-permute-start(f32[2,4,64,128]{3,2,1,0:T(8,128)S(1)} %get-tuple-element.39), channel_id=1, source_target_pairs={{0,1},{1,0},{2,3},{3,2},{4,5},{5,4},{6,7},{7,6},{8,9},{9,8},{10,11... | collective-permute-start | bytes 786440 | tf_op jit(solution)/shard_map/ppermute | solution.py:503
